TPU v7x, 256 devices: a whole 4x4x8 slice. The times are simulated.
256 devices in a mesh: front: 4 (over y), pivot: 8 (over x, core), rows: 8 (over z).
Axes of the slice: x: 4, y: 4, z: 8, core: 2. Of those that a mesh axis runs over, the one named last changes fastest.
Arguments:
- factor: float32 [4, 8, 1024, 8192], P('front', 'pivot', 'rows'), may hold values from -0.0625 to 0.0625
- inv_diag: float32 [4, 8, 1024, 1024], P('front', 'pivot', 'rows'), may hold values from -0.1875 to 0.1875
- boundary: float32 [4, 8192, 8192], P('front', ('pivot', 'rows')), may hold values from -0.0625 to 0.0625
- rhs: float32 [4, 240, 8192], P('front', None, ('pivot', 'rows')), may hold values from -6 to 6
- boundary_rhs: float32 [4, 240, 8192], P('front', None, ('pivot', 'rows')), may hold values from -6 to 6
- owner: int32 [4, 8192, 1], P('front', ('pivot', 'rows')), may hold values from 0 to 63; in each aligned block of 128 rows (0 to 127, 128 to 255, ..., all dimensions but the last counted through in order) at most 4 rows name the same one
- slot: int32 [4, 8192], P('front', ('pivot', 'rows')), may hold values from 0 to 255
- parent_in: float32 [240, 16384], P(None, ('pivot', 'rows')), may hold values from -6 to 6
Outputs:
- solution: float32 [4, 240, 8192], P('front', None, ('pivot', 'rows'))
- parent_rhs: float32 [240, 16384], P(None, ('pivot', 'rows'))
Inputs may be any that keep to these rules, and one draw needn't show every extreme that they name: Within the 128 boundary rows of one device no owner is named more than 4 times, and in every draw some device's rows name some owner exactly 4 times.
All inputs are finite; a program needn't handle non-finite values.
Results may differ from a plain program's by a relative error of at most 0.0001.
Values sent between devices are 32-bit elements; how exact they have to be, the bound alone decides.
A program may use at most 64 MiB of HBM per device.

v0:
```python
import jax
import jax.numpy as jnp
from jax import lax
from jax.sharding import PartitionSpec as P

highest = lax.Precision.HIGHEST


def shards(factor, inv_diag, boundary, rhs, boundary_rhs, owner, slot, parent_in):
    factor_rows = factor[0, 0]
    inv_rows = inv_diag[0, 0]
    bound_rows = boundary[0]
    local_rhs = rhs[0]
    local_brhs = boundary_rhs[0]
    block_count = lax.axis_size("pivot")
    row_count = lax.axis_size("rows")
    block_span = inv_rows.shape[1]
    slice_rows = factor_rows.shape[0]
    sources = local_rhs.shape[0]
    own_block = lax.axis_index("pivot")
    own_row = lax.axis_index("rows")
    contract = (((1,), (1,)), ((), ()))

    def solve_section(section_idx, carry):
        running, boundary_sum, own_solved = carry
        residual = local_rhs - running
        partial_value = jnp.dot(
            residual, inv_rows, precision=highest, preferred_element_type=jnp.float32
        )
        masked = jnp.where(own_block == section_idx, partial_value, 0.0)
        solved = lax.psum(masked, ("pivot", "rows"))
        pivot_tile = lax.dynamic_slice_in_dim(factor_rows, section_idx * block_span, block_span, 1)
        update_term = lax.dot_general(
            solved, pivot_tile, contract, precision=highest, preferred_element_type=jnp.float32
        )
        running = running + jnp.where(section_idx < own_block, update_term, 0.0)
        bound_tile = lax.dynamic_slice_in_dim(bound_rows, section_idx * block_span, block_span, 1)
        boundary_sum = boundary_sum + lax.dot_general(
            solved, bound_tile, contract, precision=highest, preferred_element_type=jnp.float32
        )
        own_piece = lax.dynamic_slice_in_dim(solved, own_row * slice_rows, slice_rows, 1)
        own_solved = jnp.where(own_block == section_idx, own_piece, own_solved)
        return (running, boundary_sum, own_solved)

    start = (
        jnp.zeros((sources, slice_rows), jnp.float32),
        jnp.zeros((sources, bound_rows.shape[0]), jnp.float32),
        jnp.zeros((sources, slice_rows), jnp.float32),
    )
    running, boundary_sum, own_solved = lax.fori_loop(0, block_count, solve_section, start)
    update = local_brhs - boundary_sum
    out_rows = update.T
    owners = owner[0, :, 0]
    slot_ids = slot[0]
    owner_count = block_count * row_count
    capacity = max(2, 2 * out_rows.shape[0] // owner_count)
    onehot = (owners[:, None] == jnp.arange(owner_count, dtype=jnp.int32)[None, :]).astype(
        jnp.int32
    )
    before = jnp.cumsum(onehot, axis=0) - onehot
    position = jnp.sum(before * onehot, axis=1)
    dest_slot = owners * capacity + position
    select = dest_slot[None, :] == jnp.arange(owner_count * capacity, dtype=jnp.int32)[:, None]
    send_rows = jnp.dot(
        select.astype(jnp.float32), out_rows, precision=highest, preferred_element_type=jnp.float32
    )
    send_slot = jnp.max(jnp.where(select, slot_ids[None, :], -1), axis=1)
    got_rows, got_slots = (
        lax.all_to_all(
            send_rows.reshape(owner_count, capacity, sources),
            ("pivot", "rows"),
            split_axis=0,
            concat_axis=0,
            tiled=True,
        ),
        lax.all_to_all(
            send_slot.reshape(owner_count, capacity),
            ("pivot", "rows"),
            split_axis=0,
            concat_axis=0,
            tiled=True,
        ),
    )
    got_rows = got_rows.reshape(owner_count * capacity, sources)
    got_slots = got_slots.reshape(owner_count * capacity)
    parent_rows = parent_in.shape[1]
    slot_hits = (got_slots[:, None] == jnp.arange(parent_rows, dtype=jnp.int32)[None, :]).astype(
        jnp.float32
    )
    local_part = jnp.einsum(
        "ks,ko->so", got_rows, slot_hits, precision=highest, preferred_element_type=jnp.float32
    )
    sibling_total = lax.psum(local_part, "front")
    parent = parent_in + sibling_total
    return (own_solved[None], parent)


def solution(mesh):
    placed = (
        P("front", "pivot", "rows", None),
        P("front", "pivot", "rows", None),
        P("front", ("pivot", "rows"), None),
        P("front", None, ("pivot", "rows")),
        P("front", None, ("pivot", "rows")),
        P("front", ("pivot", "rows"), None),
        P("front", ("pivot", "rows")),
        P(None, ("pivot", "rows")),
    )
    return jax.shard_map(
        shards,
        mesh=mesh,
        in_specs=placed,
        out_specs=(P("front", None, ("pivot", "rows")), P(None, ("pivot", "rows"))),
        check_vma=False,
    )
```

profile of v0, /device:TPU:2, one launch (start us, length us, event | category | flops | bytes accessed | tf_op | source)
XLA Modules:
  0.0 1667.7 jit_solution(10472206007967670768)
XLA Ops:
  11.9 12.0 all-to-all-start.1
  24.0 1568.2 %while.20 = (s32[]{:T(128)}, f32[240,128]{1,0:T(8,128)S(1)}, f32[240,128]{1,0:T(8,128)S(1)}, f32[240,128]{1,0:T(8,128)S(1)}, s32[]{:T(128)}, /*index=5*/f32[240,...) while((s32[]{:T(128)}, f32[240,128]{1,0:T(8,128)S(1)}, ...), condition=%wide.region_2.3_spmd.clone, body=%wide.region_0.2_spmd.clone.sunk | while | flops 1133230080 | bytes 11526409 | solution.py:50
  24.1 3.1 convolution_select_fusion.3
  27.2 189.0 %all-reduce.5.cloned.1.call-done = f32[240,1024]{1,0:T(8,128)} async-done(((f32[240,1024]{1,0:T(8,128)}), f32[240,1024]{1,0:T(8,128)}) %all-reduce.5.cloned.1.call-update) | async-done | bytes 983056 | tf_op jit(solution)/shard_map/while/body/eval_jaxpr/psum | solution.py:31
  221.9 3.0 convolution_select_fusion.3
  224.9 187.0 %all-reduce.5.cloned.1.call-done = f32[240,1024]{1,0:T(8,128)} async-done(((f32[240,1024]{1,0:T(8,128)}), f32[240,1024]{1,0:T(8,128)}) %all-reduce.5.cloned.1.call-update) | async-done | bytes 983056 | tf_op jit(solution)/shard_map/while/body/eval_jaxpr/psum | solution.py:31
  417.6 3.0 convolution_select_fusion.3
  420.7 187.0 %all-reduce.5.cloned.1.call-done = f32[240,1024]{1,0:T(8,128)} async-done(((f32[240,1024]{1,0:T(8,128)}), f32[240,1024]{1,0:T(8,128)}) %all-reduce.5.cloned.1.call-update) | async-done | bytes 983056 | tf_op jit(solution)/shard_map/while/body/eval_jaxpr/psum | solution.py:31
  607.7 2.3 convolution_add_fusion.2
  613.3 3.0 convolution_select_fusion.3
  616.4 186.7 %all-reduce.5.cloned.1.call-done = f32[240,1024]{1,0:T(8,128)} async-done(((f32[240,1024]{1,0:T(8,128)}), f32[240,1024]{1,0:T(8,128)}) %all-reduce.5.cloned.1.call-update) | async-done | bytes 983056 | tf_op jit(solution)/shard_map/while/body/eval_jaxpr/psum | solution.py:31
  808.7 3.0 convolution_select_fusion.3
  811.8 186.7 %all-reduce.5.cloned.1.call-done = f32[240,1024]{1,0:T(8,128)} async-done(((f32[240,1024]{1,0:T(8,128)}), f32[240,1024]{1,0:T(8,128)}) %all-reduce.5.cloned.1.call-update) | async-done | bytes 983056 | tf_op jit(solution)/shard_map/while/body/eval_jaxpr/psum | solution.py:31
  1004.2 3.0 convolution_select_fusion.3
  1007.2 187.4 %all-reduce.5.cloned.1.call-done = f32[240,1024]{1,0:T(8,128)} async-done(((f32[240,1024]{1,0:T(8,128)}), f32[240,1024]{1,0:T(8,128)}) %all-reduce.5.cloned.1.call-update) | async-done | bytes 983056 | tf_op jit(solution)/shard_map/while/body/eval_jaxpr/psum | solution.py:31
  1194.6 2.3 convolution_add_fusion.2
  1200.3 3.0 convolution_select_fusion.3
  1203.4 187.4 %all-reduce.5.cloned.1.call-done = f32[240,1024]{1,0:T(8,128)} async-done(((f32[240,1024]{1,0:T(8,128)}), f32[240,1024]{1,0:T(8,128)}) %all-reduce.5.cloned.1.call-update) | async-done | bytes 983056 | tf_op jit(solution)/shard_map/while/body/eval_jaxpr/psum | solution.py:31
  1396.5 3.0 convolution_select_fusion.3
  1399.6 187.0 %all-reduce.5.cloned.1.call-done = f32[240,1024]{1,0:T(8,128)} async-done(((f32[240,1024]{1,0:T(8,128)}), f32[240,1024]{1,0:T(8,128)}) %all-reduce.5.cloned.1.call-update) | async-done | bytes 983056 | tf_op jit(solution)/shard_map/while/body/eval_jaxpr/psum | solution.py:31
  1586.6 2.3 convolution_add_fusion.2
  1593.3 8.3 all-to-all-start
  1603.0 11.3 all-to-all-done
  1615.6 43.0 %all-reduce.3.cloned.1.call-done = f32[240,256]{1,0:T(8,128)} async-done(((f32[240,256]{1,0:T(8,128)}), f32[240,256]{1,0:T(8,128)}) %all-reduce.3.cloned.1.call-update) | async-done | bytes 245776 | tf_op jit(solution)/shard_map/psum | solution.py:93
  (63 shorter events, 47.4 us)
Async XLA Ops:
  11.9 1581.4 %all-to-all-start.1 = ((s32[64,1,4]{2,1,0:T(1,128)}), s32[64,1,4]{2,1,0:T(1,128)S(1)}, u32[]{:S(2)}, u32[]{:S(2)}) async-start(s32[64,1,4]{2,1,0:T(1,128)} %bitcast.8), calls=%async_computation.1 | async-start | bytes 65536 | tf_op jit(solution)/shard_map/all_to_all | solution.py:76
  24.0 1568.2 %copy-start.2 = (f32[1,240,128]{2,1,0:T(8,128)S(1)}, f32[1,240,128]{2,1,0:T(8,128)}, u32[]{:S(2)}) copy-start(f32[1,240,128]{2,1,0:T(8,128)} %param.14) | copy-start | bytes 368644
  24.0 1634.6 %copy-start.1 = (f32[240,256]{1,0:T(8,128)S(1)}, f32[240,256]{1,0:T(8,128)}, u32[]{:S(2)}) copy-start(f32[240,256]{1,0:T(8,128)} %param.17) | copy-start | bytes 737284
  24.0 192.2 %all-reduce.5.cloned.1.call-start = ((), (), s32[]{:S(2)}) async-start(), calls=%async_computation.3 | async-start | bytes 1966080 | tf_op jit(solution)/shard_map/while/body/eval_jaxpr/psum | solution.py:31
  221.8 190.1 %all-reduce.5.cloned.1.call-start = ((), (), s32[]{:S(2)}) async-start(), calls=%async_computation.3 | async-start | bytes 1966080 | tf_op jit(solution)/shard_map/while/body/eval_jaxpr/psum | solution.py:31
  417.6 190.1 %all-reduce.5.cloned.1.call-start = ((), (), s32[]{:S(2)}) async-start(), calls=%async_computation.3 | async-start | bytes 1966080 | tf_op jit(solution)/shard_map/while/body/eval_jaxpr/psum | solution.py:31
  613.3 189.8 %all-reduce.5.cloned.1.call-start = ((), (), s32[]{:S(2)}) async-start(), calls=%async_computation.3 | async-start | bytes 1966080 | tf_op jit(solution)/shard_map/while/body/eval_jaxpr/psum | solution.py:31
  808.7 189.8 %all-reduce.5.cloned.1.call-start = ((), (), s32[]{:S(2)}) async-start(), calls=%async_computation.3 | async-start | bytes 1966080 | tf_op jit(solution)/shard_map/while/body/eval_jaxpr/psum | solution.py:31
  1004.1 190.5 %all-reduce.5.cloned.1.call-start = ((), (), s32[]{:S(2)}) async-start(), calls=%async_computation.3 | async-start | bytes 1966080 | tf_op jit(solution)/shard_map/while/body/eval_jaxpr/psum | solution.py:31
  1200.3 190.6 %all-reduce.5.cloned.1.call-start = ((), (), s32[]{:S(2)}) async-start(), calls=%async_computation.3 | async-start | bytes 1966080 | tf_op jit(solution)/shard_map/while/body/eval_jaxpr/psum | solution.py:31
  1396.4 190.2 %all-reduce.5.cloned.1.call-start = ((), (), s32[]{:S(2)}) async-start(), calls=%async_computation.3 | async-start | bytes 1966080 | tf_op jit(solution)/shard_map/while/body/eval_jaxpr/psum | solution.py:31
  1592.2 68.1 %copy-start = (f32[240,128]{1,0:T(8,128)}, f32[240,128]{1,0:T(8,128)S(1)}, u32[]{:S(2)}) copy-start(f32[240,128]{1,0:T(8,128)S(1)} %get-tuple-element.239) | copy-start | bytes 368644
  1593.3 21.0 %all-to-all-start = ((f32[64,4,240]{2,1,0:T(4,128)}), f32[64,4,240]{2,1,0:T(4,128)S(1)}, u32[]{:S(2)}, u32[]{:S(2)}) async-start(f32[64,4,240]{2,1,0:T(4,128)} %reshape.25), calls=%async_computation | async-start | bytes 524288 | tf_op jit(solution)/shard_map/all_to_all | solution.py:69
  1601.6 56.9 %all-reduce.3.cloned.1.call-start = ((), (), s32[]{:S(2)}) async-start(), calls=%async_computation.2 | async-start | bytes 491520 | tf_op jit(solution)/shard_map/psum | solution.py:93
Sparse Core Ops, SparseCore 0:
  28.2 187.9 all-reduce.4
  226.0 185.8 all-reduce.4
  421.7 185.8 all-reduce.4
  617.2 185.8 all-reduce.4
  812.6 185.8 all-reduce.4
  1008.0 186.6 all-reduce.4
  1204.5 186.3 all-reduce.4
  1400.6 185.9 all-reduce.4
Sparse Core Ops, SparseCore 1:
  1615.7 42.8 all-reduce.2
where the time goes:
time: 1670 us
  waiting for transfers between devices  1550 us (93%)
  matrix products  62.8 us (4%)
  starting transfers between devices  20.7 us (1%)
    psum x8, waiting for transfers between devices, solve_section(): solved = lax.psum(masked, ('pivot', 'rows'))  1500 us
    psum x1, waiting for transfers between devices, shards(): sibling_total = lax.psum(local_part, 'front')  43 us
  transfers between devices with their start and end apart: 11, of which 10 were waited for; matrix products, arithmetic and copies ran while one was open for 4% of the time, Pallas kernels for 0%

commit v1 on v0

--- a/solution.py
+++ b/solution.py
@@ -4,6 +4,10 @@
 from jax.sharding import PartitionSpec as P
 
 highest = lax.Precision.HIGHEST
+
+
+def build_strings_here(tile_in):
+    return lax.psum(lax.psum(tile_in, axis_name="rows"), axis_name="pivot")
 
 
 def shards(factor, inv_diag, boundary, rhs, boundary_rhs, owner, slot, parent_in):
@@ -28,7 +32,7 @@
             residual, inv_rows, precision=highest, preferred_element_type=jnp.float32
         )
         masked = jnp.where(own_block == section_idx, partial_value, 0.0)
-        solved = lax.psum(masked, ("pivot", "rows"))
+        solved = build_strings_here(masked)
         pivot_tile = lax.dynamic_slice_in_dim(factor_rows, section_idx * block_span, block_span, 1)
         update_term = lax.dot_general(
             solved, pivot_tile, contract, precision=highest, preferred_element_type=jnp.float32

time: 1670 us -> 1320 us (0.79)
  waiting for transfers between devices: 1550 us -> 1200 us
    psum x8 -> x16, waiting for transfers between devices: 1500 us -> 1140 us  [build_strings_here(): return lax.psum(lax.psum(tile_in, axis_name='rows'), axis_name='pivot')]
  transfers between devices with their start and end apart: 11 -> 19, of which waited for: 10 -> 18; matrix products, arithmetic and copies ran while one was open for 4% -> 5% of each run, Pallas kernels for 0% -> 0%
where the time goes in v1:
time: 1320 us
  waiting for transfers between devices  1200 us (91%)
  matrix products  62.8 us (5%)
  starting transfers between devices  23.6 us (2%)
  between operations  15.3 us (1%)
    psum x16, waiting for transfers between devices, build_strings_here(): return lax.psum(lax.psum(tile_in, axis_name='rows'), axis_name='pivot')  1140 us
    psum x1, waiting for transfers between devices, shards(): sibling_total = lax.psum(local_part, 'front')  43 us
  transfers between devices with their start and end apart: 19, of which 18 were waited for; matrix products, arithmetic and copies ran while one was open for 5% of the time, Pallas kernels for 0%

profile of v1, /device:TPU:2, one launch (start us, length us, event | category | flops | bytes accessed | tf_op | source)
XLA Modules:
  0.0 1317.2 jit_solution(12579974911695049596)
XLA Ops:
  11.9 12.0 all-to-all-start.1
  24.0 1215.5 %while.20 = (s32[]{:T(128)}, f32[240,128]{1,0:T(8,128)S(1)}, f32[240,128]{1,0:T(8,128)S(1)}, f32[240,128]{1,0:T(8,128)S(1)}, s32[]{:T(128)}, /*index=5*/f32[240,...) while((s32[]{:T(128)}, f32[240,128]{1,0:T(8,128)S(1)}, ...), condition=%wide.region_3.4_spmd.clone, body=%wide.region_0.3_spmd.clone.sunk | while | flops 1133475840 | bytes 17424688 | solution.py:54
  24.1 3.1 convolution_select_fusion.3
  27.2 76.9 %all-reduce.6.cloned.1.call-done = f32[240,1024]{1,0:T(8,128)} async-done(((f32[240,1024]{1,0:T(8,128)}), f32[240,1024]{1,0:T(8,128)}) %all-reduce.6.cloned.1.call-update) | async-done | bytes 983056 | tf_op jit(solution)/shard_map/while/body/eval_jaxpr/psum | solution.py:10
  104.2 66.0 %all-reduce.8.cloned.1.call-done = f32[240,1024]{1,0:T(8,128)} async-done(((f32[240,1024]{1,0:T(8,128)}), f32[240,1024]{1,0:T(8,128)}) %all-reduce.8.cloned.1.call-update) | async-done | bytes 983056 | tf_op jit(solution)/shard_map/while/body/eval_jaxpr/psum | solution.py:10
  179.0 77.2 %all-reduce.6.cloned.1.call-done = f32[240,1024]{1,0:T(8,128)} async-done(((f32[240,1024]{1,0:T(8,128)}), f32[240,1024]{1,0:T(8,128)}) %all-reduce.6.cloned.1.call-update) | async-done | bytes 983056 | tf_op jit(solution)/shard_map/while/body/eval_jaxpr/psum | solution.py:10
  256.3 65.9 %all-reduce.8.cloned.1.call-done = f32[240,1024]{1,0:T(8,128)} async-done(((f32[240,1024]{1,0:T(8,128)}), f32[240,1024]{1,0:T(8,128)}) %all-reduce.8.cloned.1.call-update) | async-done | bytes 983056 | tf_op jit(solution)/shard_map/while/body/eval_jaxpr/psum | solution.py:10
  330.9 77.3 %all-reduce.6.cloned.1.call-done = f32[240,1024]{1,0:T(8,128)} async-done(((f32[240,1024]{1,0:T(8,128)}), f32[240,1024]{1,0:T(8,128)}) %all-reduce.6.cloned.1.call-update) | async-done | bytes 983056 | tf_op jit(solution)/shard_map/while/body/eval_jaxpr/psum | solution.py:10
  408.2 65.9 %all-reduce.8.cloned.1.call-done = f32[240,1024]{1,0:T(8,128)} async-done(((f32[240,1024]{1,0:T(8,128)}), f32[240,1024]{1,0:T(8,128)}) %all-reduce.8.cloned.1.call-update) | async-done | bytes 983056 | tf_op jit(solution)/shard_map/while/body/eval_jaxpr/psum | solution.py:10
  482.9 77.2 %all-reduce.6.cloned.1.call-done = f32[240,1024]{1,0:T(8,128)} async-done(((f32[240,1024]{1,0:T(8,128)}), f32[240,1024]{1,0:T(8,128)}) %all-reduce.6.cloned.1.call-update) | async-done | bytes 983056 | tf_op jit(solution)/shard_map/while/body/eval_jaxpr/psum | solution.py:10
  560.1 66.0 %all-reduce.8.cloned.1.call-done = f32[240,1024]{1,0:T(8,128)} async-done(((f32[240,1024]{1,0:T(8,128)}), f32[240,1024]{1,0:T(8,128)}) %all-reduce.8.cloned.1.call-update) | async-done | bytes 983056 | tf_op jit(solution)/shard_map/while/body/eval_jaxpr/psum | solution.py:10
  634.9 77.3 %all-reduce.6.cloned.1.call-done = f32[240,1024]{1,0:T(8,128)} async-done(((f32[240,1024]{1,0:T(8,128)}), f32[240,1024]{1,0:T(8,128)}) %all-reduce.6.cloned.1.call-update) | async-done | bytes 983056 | tf_op jit(solution)/shard_map/while/body/eval_jaxpr/psum | solution.py:10
  712.3 65.8 %all-reduce.8.cloned.1.call-done = f32[240,1024]{1,0:T(8,128)} async-done(((f32[240,1024]{1,0:T(8,128)}), f32[240,1024]{1,0:T(8,128)}) %all-reduce.8.cloned.1.call-update) | async-done | bytes 983056 | tf_op jit(solution)/shard_map/while/body/eval_jaxpr/psum | solution.py:10
  783.8 3.0 convolution_select_fusion.3
  786.9 77.3 %all-reduce.6.cloned.1.call-done = f32[240,1024]{1,0:T(8,128)} async-done(((f32[240,1024]{1,0:T(8,128)}), f32[240,1024]{1,0:T(8,128)}) %all-reduce.6.cloned.1.call-update) | async-done | bytes 983056 | tf_op jit(solution)/shard_map/while/body/eval_jaxpr/psum | solution.py:10
  864.2 65.9 %all-reduce.8.cloned.1.call-done = f32[240,1024]{1,0:T(8,128)} async-done(((f32[240,1024]{1,0:T(8,128)}), f32[240,1024]{1,0:T(8,128)}) %all-reduce.8.cloned.1.call-update) | async-done | bytes 983056 | tf_op jit(solution)/shard_map/while/body/eval_jaxpr/psum | solution.py:10
  938.8 77.3 %all-reduce.6.cloned.1.call-done = f32[240,1024]{1,0:T(8,128)} async-done(((f32[240,1024]{1,0:T(8,128)}), f32[240,1024]{1,0:T(8,128)}) %all-reduce.6.cloned.1.call-update) | async-done | bytes 983056 | tf_op jit(solution)/shard_map/while/body/eval_jaxpr/psum | solution.py:10
  1016.1 65.9 %all-reduce.8.cloned.1.call-done = f32[240,1024]{1,0:T(8,128)} async-done(((f32[240,1024]{1,0:T(8,128)}), f32[240,1024]{1,0:T(8,128)}) %all-reduce.8.cloned.1.call-update) | async-done | bytes 983056 | tf_op jit(solution)/shard_map/while/body/eval_jaxpr/psum | solution.py:10
  1087.6 3.0 convolution_select_fusion.3
  1090.7 77.3 %all-reduce.6.cloned.1.call-done = f32[240,1024]{1,0:T(8,128)} async-done(((f32[240,1024]{1,0:T(8,128)}), f32[240,1024]{1,0:T(8,128)}) %all-reduce.6.cloned.1.call-update) | async-done | bytes 983056 | tf_op jit(solution)/shard_map/while/body/eval_jaxpr/psum | solution.py:10
  1168.1 65.9 %all-reduce.8.cloned.1.call-done = f32[240,1024]{1,0:T(8,128)} async-done(((f32[240,1024]{1,0:T(8,128)}), f32[240,1024]{1,0:T(8,128)}) %all-reduce.8.cloned.1.call-update) | async-done | bytes 983056 | tf_op jit(solution)/shard_map/while/body/eval_jaxpr/psum | solution.py:10
  1240.6 10.8 all-to-all-start
  1252.9 11.3 all-to-all-done
  1265.4 43.0 %all-reduce.4.cloned.1.call-done = f32[240,256]{1,0:T(8,128)} async-done(((f32[240,256]{1,0:T(8,128)}), f32[240,256]{1,0:T(8,128)}) %all-reduce.4.cloned.1.call-update) | async-done | bytes 245776 | tf_op jit(solution)/shard_map/psum | solution.py:97
  (87 shorter events, 70.0 us)
Async XLA Ops:
  11.9 1228.7 %all-to-all-start.1 = ((s32[64,1,4]{2,1,0:T(1,128)}), s32[64,1,4]{2,1,0:T(1,128)S(1)}, u32[]{:S(2)}, u32[]{:S(2)}) async-start(s32[64,1,4]{2,1,0:T(1,128)} %bitcast.8), calls=%async_computation.1 | async-start | bytes 65536 | tf_op jit(solution)/shard_map/all_to_all | solution.py:80
  24.0 1215.5 %copy-start.2 = (f32[1,240,128]{2,1,0:T(8,128)S(1)}, f32[1,240,128]{2,1,0:T(8,128)}, u32[]{:S(2)}) copy-start(f32[1,240,128]{2,1,0:T(8,128)} %param.14) | copy-start | bytes 368644
  24.0 1284.4 %copy-start.1 = (f32[240,256]{1,0:T(8,128)S(1)}, f32[240,256]{1,0:T(8,128)}, u32[]{:S(2)}) copy-start(f32[240,256]{1,0:T(8,128)} %param.17) | copy-start | bytes 737284
  24.0 80.2 %all-reduce.6.cloned.1.call-start = ((), (), s32[]{:S(2)}) async-start(), calls=%async_computation.3 | async-start | bytes 1966080 | tf_op jit(solution)/shard_map/while/body/eval_jaxpr/psum | solution.py:10
  27.2 143.0 %all-reduce.8.cloned.1.call-start = ((), (), s32[]{:S(2)}) async-start(), calls=%async_computation.4 | async-start | bytes 1966080 | tf_op jit(solution)/shard_map/while/body/eval_jaxpr/psum | solution.py:10
  175.8 80.4 %all-reduce.6.cloned.1.call-start = ((), (), s32[]{:S(2)}) async-start(), calls=%async_computation.3 | async-start | bytes 1966080 | tf_op jit(solution)/shard_map/while/body/eval_jaxpr/psum | solution.py:10
  178.9 143.2 %all-reduce.8.cloned.1.call-start = ((), (), s32[]{:S(2)}) async-start(), calls=%async_computation.4 | async-start | bytes 1966080 | tf_op jit(solution)/shard_map/while/body/eval_jaxpr/psum | solution.py:10
  327.7 80.5 %all-reduce.6.cloned.1.call-start = ((), (), s32[]{:S(2)}) async-start(), calls=%async_computation.3 | async-start | bytes 1966080 | tf_op jit(solution)/shard_map/while/body/eval_jaxpr/psum | solution.py:10
  330.8 143.3 %all-reduce.8.cloned.1.call-start = ((), (), s32[]{:S(2)}) async-start(), calls=%async_computation.4 | async-start | bytes 1966080 | tf_op jit(solution)/shard_map/while/body/eval_jaxpr/psum | solution.py:10
  479.7 80.4 %all-reduce.6.cloned.1.call-start = ((), (), s32[]{:S(2)}) async-start(), calls=%async_computation.3 | async-start | bytes 1966080 | tf_op jit(solution)/shard_map/while/body/eval_jaxpr/psum | solution.py:10
  482.8 143.3 %all-reduce.8.cloned.1.call-start = ((), (), s32[]{:S(2)}) async-start(), calls=%async_computation.4 | async-start | bytes 1966080 | tf_op jit(solution)/shard_map/while/body/eval_jaxpr/psum | solution.py:10
  631.7 80.5 %all-reduce.6.cloned.1.call-start = ((), (), s32[]{:S(2)}) async-start(), calls=%async_computation.3 | async-start | bytes 1966080 | tf_op jit(solution)/shard_map/while/body/eval_jaxpr/psum | solution.py:10
  634.8 143.3 %all-reduce.8.cloned.1.call-start = ((), (), s32[]{:S(2)}) async-start(), calls=%async_computation.4 | async-start | bytes 1966080 | tf_op jit(solution)/shard_map/while/body/eval_jaxpr/psum | solution.py:10
  783.7 80.4 %all-reduce.6.cloned.1.call-start = ((), (), s32[]{:S(2)}) async-start(), calls=%async_computation.3 | async-start | bytes 1966080 | tf_op jit(solution)/shard_map/while/body/eval_jaxpr/psum | solution.py:10
  786.8 143.2 %all-reduce.8.cloned.1.call-start = ((), (), s32[]{:S(2)}) async-start(), calls=%async_computation.4 | async-start | bytes 1966080 | tf_op jit(solution)/shard_map/while/body/eval_jaxpr/psum | solution.py:10
  935.7 80.4 %all-reduce.6.cloned.1.call-start = ((), (), s32[]{:S(2)}) async-start(), calls=%async_computation.3 | async-start | bytes 1966080 | tf_op jit(solution)/shard_map/while/body/eval_jaxpr/psum | solution.py:10
  938.8 143.2 %all-reduce.8.cloned.1.call-start = ((), (), s32[]{:S(2)}) async-start(), calls=%async_computation.4 | async-start | bytes 1966080 | tf_op jit(solution)/shard_map/while/body/eval_jaxpr/psum | solution.py:10
  1087.6 80.4 %all-reduce.6.cloned.1.call-start = ((), (), s32[]{:S(2)}) async-start(), calls=%async_computation.3 | async-start | bytes 1966080 | tf_op jit(solution)/shard_map/while/body/eval_jaxpr/psum | solution.py:10
  1090.7 143.2 %all-reduce.8.cloned.1.call-start = ((), (), s32[]{:S(2)}) async-start(), calls=%async_computation.4 | async-start | bytes 1966080 | tf_op jit(solution)/shard_map/while/body/eval_jaxpr/psum | solution.py:10
  1239.5 70.6 %copy-start = (f32[240,128]{1,0:T(8,128)}, f32[240,128]{1,0:T(8,128)S(1)}, u32[]{:S(2)}) copy-start(f32[240,128]{1,0:T(8,128)S(1)} %get-tuple-element.239) | copy-start | bytes 368644
  1240.6 23.5 %all-to-all-start = ((f32[64,4,240]{2,1,0:T(4,128)}), f32[64,4,240]{2,1,0:T(4,128)S(1)}, u32[]{:S(2)}, u32[]{:S(2)}) async-start(f32[64,4,240]{2,1,0:T(4,128)} %reshape.25), calls=%async_computation | async-start | bytes 524288 | tf_op jit(solution)/shard_map/all_to_all | solution.py:73
  1251.5 56.9 %all-reduce.4.cloned.1.call-start = ((), (), s32[]{:S(2)}) async-start(), calls=%async_computation.2 | async-start | bytes 491520 | tf_op jit(solution)/shard_map/psum | solution.py:97
Sparse Core Ops, SparseCore 0:
  27.3 76.8 all-reduce.5
  106.5 63.6 all-reduce.7
  179.0 77.1 all-reduce.5
  258.4 63.6 all-reduce.7
  330.9 77.2 all-reduce.5
  410.4 63.6 all-reduce.7
  482.9 77.1 all-reduce.5
  562.5 63.6 all-reduce.7
  635.0 77.2 all-reduce.5
  714.4 63.6 all-reduce.7
  787.0 77.1 all-reduce.5
  866.4 63.6 all-reduce.7
  938.9 77.1 all-reduce.5
  1018.3 63.6 all-reduce.7
  1090.8 77.1 all-reduce.5
  1170.2 63.6 all-reduce.7
Sparse Core Ops, SparseCore 1:
  1265.5 42.9 all-reduce.3
